TPU v7x, 32 devices: a whole 2x2x4 slice. The times are simulated.
32 devices in a mesh: ent: 16 (over z, y, x), rep: 2 (over core).
Axes of the slice: x: 2, y: 2, z: 4, core: 2. Of those that a mesh axis runs over, the one named last changes fastest.
Arguments:
- head_ids: int32 [8192], P(('ent', 'rep')), may hold values from 0 to 32767, as said below
- rel_ids: int32 [8192], P(('ent', 'rep')), may hold values from 0 to 4095
- tail_ids: int32 [8192], P(('ent', 'rep')), may hold values from 0 to 32767, as said below
- neg_ids: int32 [256], P('ent'), may hold values from 0 to 32767, as said below
- slot_of: int32 [32768], replicated, may hold values from 0 to 32767, as said below
- relations: bfloat16 [4096, 400], replicated, may hold values from -3 to 3
- embeddings: float32 [32768, 400], P('ent'), may hold values from -1.75 to 1.75
- accumulator: float32 [32768], P('ent'), may hold values from 0.001 to 0.03
Outputs:
- new_embeddings: float32 [32768, 400], P('ent')
- new_accumulator: float32 [32768], P('ent')
Inputs may be any that keep to these rules, and one draw needn't show every extreme that they name: A permutation: every table row stores exactly one entity; the owner of entity e is slot_of[e] // 2048. `head_ids`: among the 512 endpoints (heads and tails together) of the edges of one device, at most 64 have any one owner; in every draw one owner has exactly 64 endpoints of every device. `tail_ids`: see head_ids: the bound counts heads and tails of one device together. `neg_ids`: entry j has owner j // 16.
All inputs are finite; a program needn't handle non-finite values.
Results may differ from a plain program's by a relative error of at most 0.0031.
Values may be sent and summed in bfloat16 or wider, within the bound.
No kernel may reach another device: no remote copies, remote signals or barrier semaphores. Data moves between devices by JAX's collectives and lax.ppermute only.
A program may use at most 128 MiB of HBM per device.

v0:
```python
import jax
import jax.numpy as jnp
from jax import lax
from jax.sharding import PartitionSpec as P

step_rate = 0.3


def split_parts(values):
    cut = values.shape[1] // 2
    return (values[:, :cut], values[:, cut:])


def edge_terms(head_rows, rel_rows, tail_rows, neg_rows):
    head_full = head_rows.astype(jnp.float32)
    rel_full = rel_rows.astype(jnp.float32)
    tail_full = tail_rows.astype(jnp.float32)
    head_re, head_im = split_parts(head_full)
    rel_re, rel_im = split_parts(rel_full)
    tail_re, tail_im = split_parts(tail_full)
    product = jnp.concatenate(
        [head_re * rel_re - head_im * rel_im, head_re * rel_im + head_im * rel_re], axis=1
    )
    product_low = product.astype(jnp.bfloat16)
    mirror_low = jnp.concatenate(
        [rel_re * tail_re + rel_im * tail_im, rel_re * tail_im - rel_im * tail_re], axis=1
    ).astype(jnp.bfloat16)
    positive = jnp.sum(product * tail_full, axis=1)
    inner_dims = (((1,), (1,)), ((), ()))
    tail_scores = lax.dot_general(
        product_low, neg_rows, inner_dims, preferred_element_type=jnp.float32
    )
    head_scores = lax.dot_general(
        mirror_low, neg_rows, inner_dims, preferred_element_type=jnp.float32
    )
    neg_count = neg_rows.shape[0]
    pos_grad = -jax.nn.sigmoid(-positive)
    tail_weight = (jax.nn.sigmoid(tail_scores) / neg_count).astype(jnp.bfloat16)
    head_weight = (jax.nn.sigmoid(head_scores) / neg_count).astype(jnp.bfloat16)
    product_grad = (
        jnp.dot(tail_weight, neg_rows, preferred_element_type=jnp.float32)
        + pos_grad[:, None] * tail_full
    )
    mirror_grad = jnp.dot(head_weight, neg_rows, preferred_element_type=jnp.float32)
    edge_dims = (((0,), (0,)), ((), ()))
    neg_grad = lax.dot_general(
        tail_weight, product_low, edge_dims, preferred_element_type=jnp.float32
    )
    neg_grad = neg_grad + lax.dot_general(
        head_weight, mirror_low, edge_dims, preferred_element_type=jnp.float32
    )
    grad_re, grad_im = split_parts(product_grad)
    head_grad = jnp.concatenate(
        [grad_re * rel_re + grad_im * rel_im, grad_im * rel_re - grad_re * rel_im], axis=1
    )
    back_re, back_im = split_parts(mirror_grad)
    tail_grad = pos_grad[:, None] * product + jnp.concatenate(
        [back_re * rel_re - back_im * rel_im, back_re * rel_im + back_im * rel_re], axis=1
    )
    return (head_grad, tail_grad, neg_grad)


def row_update(old_rows, old_state, gradient):
    new_state = old_state + jnp.mean(gradient * gradient, axis=1)
    new_rows = old_rows - step_rate * gradient / jnp.sqrt(new_state)[:, None]
    return (new_rows, new_state)


def shards(head_ids, rel_ids, tail_ids, neg_ids, slot_of, relations, embeddings, accumulator):
    row_count = embeddings.shape[0]
    feature_count = embeddings.shape[1]
    owner_count = lax.axis_size("ent")
    edge_count = head_ids.shape[0]
    end_ids = jnp.concatenate([head_ids, tail_ids])
    end_count = end_ids.shape[0]
    capacity = 2 * end_count // owner_count
    end_slots = slot_of[end_ids]
    owner_of = end_slots // row_count
    local_row = end_slots % row_count
    sorter = jnp.argsort(owner_of, stable=True)
    sorted_owner = owner_of[sorter]
    per_owner = jnp.sum(
        (owner_of[:, None] == jnp.arange(owner_count, dtype=jnp.int32)[None, :]).astype(jnp.int32),
        axis=0,
    )
    starting = jnp.cumsum(per_owner) - per_owner
    sorted_place = (
        sorted_owner * capacity + jnp.arange(end_count, dtype=jnp.int32) - starting[sorted_owner]
    )
    placed = jnp.zeros((end_count,), jnp.int32).at[sorter].set(sorted_place)
    requests = (
        jnp.full((owner_count * capacity,), -1, jnp.int32)
        .at[placed]
        .set(local_row)
        .reshape(owner_count, capacity)
    )
    low_table = embeddings.astype(jnp.bfloat16)
    asked_rows = lax.all_to_all(requests, "ent", split_axis=0, concat_axis=0, tiled=True)
    picked = jnp.where(
        (asked_rows >= 0)[:, :, None],
        low_table[jnp.maximum(asked_rows, 0)],
        jnp.zeros((), jnp.bfloat16),
    )
    returned = lax.all_to_all(picked, "ent", split_axis=0, concat_axis=0, tiled=True)
    fetched, asked_rows = (returned, asked_rows)
    end_rows = fetched.reshape(owner_count * capacity, feature_count)[placed]
    neg_local = slot_of[neg_ids] % row_count
    own_negs = low_table[neg_local]
    neg_rows = lax.all_gather(own_negs, "ent", axis=0, tiled=True)
    rel_rows = relations[rel_ids]
    head_grad, tail_grad, neg_grad = edge_terms(
        end_rows[:edge_count], rel_rows, end_rows[edge_count:], neg_rows
    )
    neg_part = lax.psum_scatter(neg_grad, "ent", scatter_dimension=0, tiled=True)
    outgoing = (
        jnp.zeros((owner_count * capacity, feature_count), jnp.float32)
        .at[placed]
        .set(jnp.concatenate([head_grad, tail_grad], axis=0))
    )
    incoming = lax.all_to_all(
        outgoing.reshape(owner_count, capacity, feature_count),
        "ent",
        split_axis=0,
        concat_axis=0,
        tiled=True,
    ).reshape(-1, feature_count)
    targets = jnp.where(asked_rows >= 0, asked_rows, row_count).reshape(-1)
    partial_sum = jax.ops.segment_sum(incoming, targets, num_segments=row_count + 1)[:row_count]
    partial_sum = partial_sum.at[neg_local].add(neg_part)
    summed = lax.psum(partial_sum, "rep")
    new_rows, new_state = row_update(embeddings, accumulator, summed)
    return (new_rows, new_state)


def solution(mesh):
    placed = (
        P(("ent", "rep")),
        P(("ent", "rep")),
        P(("ent", "rep")),
        P("ent"),
        P(),
        P(),
        P("ent", None),
        P("ent"),
    )
    return jax.shard_map(
        shards, mesh=mesh, in_specs=placed, out_specs=(P("ent", None), P("ent")), check_vma=False
    )
```

profile of v0, /device:TPU:0, one launch (start us, length us, event | category | flops | bytes accessed | tf_op | source)
XLA Modules:
  0.0 261.9 jit_solution(16662489668703026024)
XLA Ops:
  7.2 0.9 compare_select_fusion.2
  8.1 3.1 %gather_fusion = s32[512]{0:T(512)S(1)} fusion(s32[32768]{0:T(1024)S(1)} %copy-done, s32[1024]{0:T(1024)S(1)} %pad_clamp_fusion.5), kind=kCustom, calls=%fused_computation | custom fusion | bytes 6144 | tf_op jit(solution)/shard_map/gather | solution.py:77
  11.2 0.1 convert_reduce_fusion
  11.4 3.8 %sort.17 = (s32[512]{0:T(512)}, s32[512]{0:T(512)S(1)}) sort(s32[512]{0:T(512)S(1)} %get-tuple-element.38, s32[512]{0:T(512)S(1)} %iota.11), dimensions={0}, to_apply=%region_0.1 | sort | flops 4608 | bytes 8192 | tf_op jit(solution)/shard_map/jit(argsort)/sort | solution.py:80
  15.1 3.5 %gather_fusion.1 = s32[512]{0:T(512)S(1)} fusion(s32[512]{0:T(512)S(1)} %get-tuple-element.38, s32[1024]{0:T(1024)S(1)} %pad_clamp_fusion.4), kind=kCustom, calls=%fused_computation.1 | custom fusion | bytes 6144 | tf_op jit(solution)/shard_map/gather | solution.py:81
  18.6 0.1 copy.45
  18.8 0.1 reduce.1
  18.9 0.7 fusion.31
  19.6 4.4 %compare_select_fusion.3 = (s32[512,1]{0,1:T(1,128)S(1)}, s32[512,1]{0,1:T(1,128)S(1)}) fusion(s32[]{:T(128)} %bitcast.14, s32[]{:T(128)} %bitcast.15, s32[]{:T(128)} %bitcast.16, s32[]{:T(128)} %bitcast.17, s32[]{:T(128)} %bitcast.18, s32[]{:T(128)} %bitcast.20, s32[]{:T(128)} %bitcast.19, s32[512,1]{0,1:T(1,128)S(1)} %bitcast.53), kind=kLoop, calls=%fused_computation.63 | loop fusion | flops 7680 | bytes 6172 | tf_op jit(solution)/shard_map/gather | solution.py:88
  24.0 0.1 compare_reduce_fusion.8
  24.0 5.7 %select_subtract_fusion = s32[512]{0:T(512)S(1)} fusion(pred[512]{0:T(512)(128)(4,1)S(1)} %get-tuple-element.20, pred[512]{0:T(512)(128)(4,1)S(1)} %get-tuple-element.19, pred[512]{0:T(512)(128)(4,1)S(1)} %get-tuple-element.18, pred[512]{0:T(512)(128)(4,1)S(1)} %get-tuple-element.17, pred[512]{0:T(512)(128)(4,1)S(1)} %get-tuple-element.16, ...), kind=kLoop, calls=%fused_computation.90 | loop fusion | flops 6144 | bytes 10788 | tf_op jit(solution)/shard_map/sub | solution.py:88
  29.7 2.4 scatter_custom_fusion
  32.2 2.4 scatter_custom_fusion.1
  34.6 0.7 all_to_all.14
  35.3 8.3 %all-to-all-start = ((s32[16,1,64]{2,1,0:T(1,128)}), s32[16,1,64]{2,1,0:T(1,128)S(1)}, u32[]{:S(2)}, u32[]{:S(2)}) async-start(s32[16,1,64]{2,1,0:T(1,128)} %all_to_all.14), calls=%async_computation | async-start | bytes 16384 | tf_op jit(solution)/shard_map/all_to_all | solution.py:98
  43.7 3.4 %copy.54 = f32[2048,400]{1,0:T(8,128)} copy(f32[2048,400]{0,1:T(8,128)S(1)} %copy-done.2) | data formatting | bytes 6553600 | tf_op args[6]
  47.0 2.5 convert_element_type.26
  49.5 1.4 all-to-all-done
  50.9 0.1 reshape.293
  51.0 4.0 %gather_fusion.2 = bf16[1024,400]{1,0:T(8,128)(2,1)S(1)} fusion(bf16[2048,400]{1,0:T(8,128)(2,1)S(1)} %convert_element_type.26, s32[1024]{0:T(1024)S(1)} %broadcast_clamp_fusion), kind=kCustom, calls=%fused_computation.2 | custom fusion | bytes 1642496 | tf_op jit(solution)/shard_map/gather | solution.py:101
  55.0 1.2 broadcast_select_fusion
  56.1 5.5 %all-to-all-start.1 = ((bf16[16,64,400]{2,1,0:T(8,128)(2,1)}), bf16[16,64,400]{2,1,0:T(8,128)(2,1)S(1)}, u32[]{:S(2)}, u32[]{:S(2)}) async-start(bf16[16,64,400]{2,1,0:T(8,128)(2,1)} %broadcast_select_fusion), calls=%async_computation.1 | async-start | bytes 2097152 | tf_op jit(solution)/shard_map/all_to_all | solution.py:104
  61.7 0.7 gather_fusion.5
  62.4 0.6 gather_fusion.6
  63.0 6.0 %copy.50 = bf16[4096,400]{1,0:T(8,128)(2,1)} copy(bf16[4096,400]{0,1:T(8,128)(2,1)} %param.13) | data formatting | bytes 6553600 | tf_op args[5]
  69.0 3.9 %gather_fusion.4 = bf16[256,400]{1,0:T(8,128)(2,1)S(1)} fusion(bf16[4096,400]{1,0:T(8,128)(2,1)} %copy.50, s32[1024]{0:T(1024)S(1)} %pad_clamp_fusion.2), kind=kCustom, calls=%fused_computation.4 | custom fusion | bytes 410624 | tf_op jit(solution)/shard_map/gather | solution.py:110
  73.0 0.1 copy.51
  73.1 42.7 %all-gather = bf16[256,400]{1,0:T(8,128)(2,1)S(1)} all-gather(bf16[16,400]{1,0:T(8,128)(2,1)S(1)} %gather_fusion.6), channel_id=2, replica_groups=mesh['ent'=16,'rep'=2] {'ent'}, dimensions={0}, use_global_device_ids=true | all-gather | bytes 217600 | tf_op jit(solution)/shard_map/all_gather | solution.py:109
  115.9 2.0 gather_fusion.3
  117.9 0.1 copy.56
  118.1 0.1 copy.57
  118.3 0.1 multiply_subtract_fusion.2
  118.3 0.1 multiply_reduce_fusion.1
  118.4 0.3 fusion.10
  118.8 0.3 convolution_add_fusion.1
  119.0 0.1 multiply_add_fusion.1
  119.2 0.2 copy-done.3
  119.4 0.4 copy-done.7
  119.8 0.3 fusion.11
  120.1 0.3 fusion.32
  120.4 0.1 multiply_subtract_fusion
  120.5 0.3 copy-done.5
  120.8 0.1 maximum_add_fusion
  120.8 0.1 pad_maximum_fusion
  120.9 0.3 copy.53
  121.3 3.6 %scatter_custom_fusion.2 = f32[1024,400]{1,0:T(8,128)} fusion(s32[512]{0:T(512)S(1)} %compare_select_fusion.9, f32[512,400]{1,0:T(8,128)S(1)} %copy.53, f32[]{:T(128)} %constant.29.clone.1), kind=kCustom, calls=%fused_computation.30 | custom fusion | bytes 1638404 | tf_op jit(solution)/shard_map/scatter | solution.py:118
  125.0 3.7 %all-to-all-start.2 = ((f32[16,64,400]{2,1,0:T(8,128)}), f32[16,64,400]{2,1,0:T(8,128)S(1)}, u32[]{:S(2)}, u32[]{:S(2)}) async-start(f32[16,64,400]{2,1,0:T(8,128)} %bitcast.30), calls=%async_computation.2 | async-start | bytes 4194304 | tf_op jit(solution)/shard_map/all_to_all | solution.py:120
  128.7 0.0 reduce-scatter.2.cloned.1.call-start
  128.8 0.3 fusion.15
  129.1 1.1 convolution_add_fusion
  130.3 0.5 broadcast.384
  130.8 0.7 reduce.22
  131.5 0.1 all_to_all.16
  131.5 37.4 %all-to-all-done.2 = f32[16,64,400]{2,1,0:T(8,128)S(1)} async-done(((f32[16,64,400]{2,1,0:T(8,128)}), f32[16,64,400]{2,1,0:T(8,128)S(1)}, u32[]{:S(2)}, u32[]{:S(2)}) %all-to-all-start.2) | async-done | bytes 1638432 | tf_op jit(solution)/shard_map/all_to_all | solution.py:120
  168.9 8.7 %scatter_custom_fusion.3 = f32[2049,400]{1,0:T(8,128)} fusion(s32[1024]{0:T(1024)S(1)} %bitcast.56, f32[1024,400]{1,0:T(8,128)S(1)} %bitcast.50, f32[]{:T(128)} %constant.29.clone.1), kind=kCustom, calls=%fused_computation.14 | custom fusion | flops 409600 | bytes 3278404 | tf_op jit(solution)/shard_map/scatter-add | solution.py:128
  177.7 4.6 %slice.95 = f32[2048,400]{1,0:T(8,128)} slice(f32[2049,400]{1,0:T(8,128)} %scatter_custom_fusion.3), slice={[0:2048], [0:400]} | slice | bytes 6553600 | tf_op jit(solution)/shard_map/slice | solution.py:128
  182.3 29.7 %reduce-scatter.2.cloned.1.call-done = f32[16,400]{1,0:T(8,128)} async-done(((f32[256,400]{1,0:T(8,128)}), f32[16,400]{1,0:T(8,128)}) %reduce-scatter.2.cloned.1.call-update) | async-done | bytes 25616 | tf_op jit(solution)/shard_map/reduce_scatter | solution.py:114
  211.9 5.0 %scatter_fusion = f32[2048,400]{1,0:T(8,128)} fusion(f32[2048,400]{1,0:T(8,128)} %slice.95, s32[16]{0:T(128)S(1)} %fusion.24, f32[16,400]{1,0:T(8,128)} %reduce-scatter.2.cloned.1.call-done), kind=kCustom, calls=%fused_computation.11 | custom fusion | flops 6400 | bytes 76864 | tf_op jit(solution)/shard_map/scatter-add | solution.py:129
  217.0 24.6 %all-reduce.2.cloned.1.call-done = f32[2048,400]{1,0:T(8,128)} async-done(((f32[2048,400]{1,0:T(8,128)}), f32[2048,400]{1,0:T(8,128)}) %all-reduce.2.cloned.1.call-update) | async-done | bytes 3276816 | tf_op jit(solution)/shard_map/psum | solution.py:130
  241.6 2.7 %multiply_reduce_fusion = f32[2048]{0:T(1024)S(1)} fusion(f32[2048,400]{1,0:T(8,128)} %all-reduce.2.cloned.1.call-done), kind=kLoop, calls=%fused_computation.13 | loop fusion | flops 1636352 | bytes 3284992 | tf_op jit(solution)/shard_map/reduce_sum | solution.py:64
  244.3 0.6 fusion.29
  244.9 0.1 copy-done.1
  245.0 4.9 %divide_subtract_fusion = f32[2048,400]{1,0:T(8,128)} fusion(f32[2048,400]{1,0:T(8,128)S(1)} %copy-done.1, f32[2048,400]{1,0:T(8,128)} %all-reduce.2.cloned.1.call-done, f32[2048]{0:T(1024)S(1)} %get-tuple-element.21), kind=kLoop, calls=%fused_computation.12 | loop fusion | flops 2457600 | bytes 9838592 | tf_op jit(solution)/shard_map/sub | solution.py:65
  249.9 5.2 %copy.55 = f32[2048,400]{0,1:T(8,128)} copy(f32[2048,400]{1,0:T(8,128)} %divide_subtract_fusion) | data formatting | bytes 6553600
  (52 shorter events, 0.5 us)
Async XLA Ops:
  7.2 0.9 copy-start
  7.2 36.5 %copy-start.2 = (f32[2048,400]{0,1:T(8,128)S(1)}, f32[2048,400]{0,1:T(8,128)}, u32[]{:S(2)}) copy-start(f32[2048,400]{0,1:T(8,128)} %param.14) | copy-start | bytes 9830404
  35.3 15.6 %all-to-all-start = ((s32[16,1,64]{2,1,0:T(1,128)}), s32[16,1,64]{2,1,0:T(1,128)S(1)}, u32[]{:S(2)}, u32[]{:S(2)}) async-start(s32[16,1,64]{2,1,0:T(1,128)} %all_to_all.14), calls=%async_computation | async-start | bytes 16384 | tf_op jit(solution)/shard_map/all_to_all | solution.py:98
  54.9 6.7 %copy-start.13 = (s32[16]{0:T(128)S(1)}, s32[16]{0:T(128)}, u32[]{:S(2)}) copy-start(s32[16]{0:T(128)} %param.11) | copy-start | bytes 196
  56.1 59.8 %all-to-all-start.1 = ((bf16[16,64,400]{2,1,0:T(8,128)(2,1)}), bf16[16,64,400]{2,1,0:T(8,128)(2,1)S(1)}, u32[]{:S(2)}, u32[]{:S(2)}) async-start(bf16[16,64,400]{2,1,0:T(8,128)(2,1)} %broadcast_select_fusion), calls=%async_computation.1 | async-start | bytes 2097152 | tf_op jit(solution)/shard_map/all_to_all | solution.py:104
  61.7 7.3 %copy-start.12 = (s32[256]{0:T(256)S(1)}, s32[256]{0:T(256)}, u32[]{:S(2)}) copy-start(s32[256]{0:T(256)} %param.9) | copy-start | bytes 3076
  118.8 0.6 copy-start.3
  119.1 0.6 copy-start.7
  119.2 0.7 copy-start.9
  120.1 0.7 copy-start.5
  121.3 7.5 %copy-start.4 = (bf16[256,256]{1,0:T(8,128)(2,1)S(1)}, bf16[256,256]{1,0:T(8,128)(2,1)}, u32[]{:S(2)}) copy-start(bf16[256,256]{1,0:T(8,128)(2,1)} %copy-done.3) | copy-start | bytes 393220
  121.3 7.7 %copy-start.6 = (bf16[256,256]{1,0:T(8,128)(2,1)S(1)}, bf16[256,256]{1,0:T(8,128)(2,1)}, u32[]{:S(2)}) copy-start(bf16[256,256]{1,0:T(8,128)(2,1)} %copy-done.5) | copy-start | bytes 393220
  121.3 7.7 %copy-start.8 = (bf16[256,200]{0,1:T(8,128)(2,1)S(1)}, bf16[256,200]{0,1:T(8,128)(2,1)}, u32[]{:S(2)}) copy-start(bf16[256,200]{0,1:T(8,128)(2,1)} %copy-done.7) | copy-start | bytes 307204
  121.3 7.7 %copy-start.10 = (bf16[256,200]{0,1:T(8,128)(2,1)S(1)}, bf16[256,200]{0,1:T(8,128)(2,1)}, u32[]{:S(2)}) copy-start(bf16[256,200]{0,1:T(8,128)(2,1)} %copy-done.9) | copy-start | bytes 307204
  125.0 44.0 %all-to-all-start.2 = ((f32[16,64,400]{2,1,0:T(8,128)}), f32[16,64,400]{2,1,0:T(8,128)S(1)}, u32[]{:S(2)}, u32[]{:S(2)}) async-start(f32[16,64,400]{2,1,0:T(8,128)} %bitcast.30), calls=%async_computation.2 | async-start | bytes 4194304 | tf_op jit(solution)/shard_map/all_to_all | solution.py:120
  128.7 83.2 %reduce-scatter.2.cloned.1.call-start = ((), (), s32[]{:S(2)}) async-start(), calls=%async_computation.4 | async-start | bytes 557056 | tf_op jit(solution)/shard_map/reduce_scatter | solution.py:114
  130.2 111.3 %all-reduce.2.cloned.1.call-start = ((), (), s32[]{:S(2)}) async-start(), calls=%async_computation.5 | async-start | bytes 8388608 | tf_op jit(solution)/shard_map/psum | solution.py:130
  217.0 27.3 %copy-start.11 = (f32[2048]{0:T(1024)S(1)}, f32[2048]{0:T(1024)}, u32[]{:S(2)}) copy-start(f32[2048]{0:T(1024)} %param.15) | copy-start | bytes 24580
  241.6 3.4 %copy-start.1 = (f32[2048,400]{1,0:T(8,128)S(1)}, f32[2048,400]{1,0:T(8,128)}, u32[]{:S(2)}) copy-start(f32[2048,400]{1,0:T(8,128)} %copy.54) | copy-start | bytes 9830404
Sparse Core Ops, SparseCore 0:
  131.8 80.1 reduce-scatter.1
  217.1 24.4 all-reduce.1
where the time goes:
time: 263 us; the launch traced here: 262 us
  waiting for transfers between devices  93.1 us (35%)
  local copies, waits for them, and re-layouts  49.5 us (19%)
  blocking collectives  42.7 us (16%)
  other arithmetic  41.9 us (16%)
  starting transfers between devices  17.7 us (7%)
  between operations  14.5 us (6%)
    all_gather x1, blocking collectives, shards(): neg_rows = lax.all_gather(own_negs, 'ent', axis=0, tiled=True)  42.7 us
    all_to_all x1, waiting for transfers between devices, shards(): lax.all_to_all(outgoing.reshape(owner_count, capacity, feature_count), 'e...  37.4 us
    reduce_scatter x1, waiting for transfers between devices, shards(): lax.psum_scatter(neg_grad, 'ent', scatter_dimension=0, tiled=True)  29.7 us
    psum x1, waiting for transfers between devices, shards(): summed = lax.psum(partial_sum, 'rep')  24.6 us
    unnamed x33, local copies, waits for them, and re-layouts  16 us
    scatter-add x1, other arithmetic, shards(): jax.ops.segment_sum(incoming, targets, num_segments=row_count + 1)  8.75 us
    all_to_all x1, starting transfers between devices, shards(): lax.all_to_all(requests, 'ent', split_axis=0, concat_axis=0, tiled=True)  8.34 us
    sub x1, other arithmetic, shards(): sorted_owner * capacity + jnp.arange(end_count, dtype=jnp.int32)  5.67 us
  transfers between devices with their start and end apart: 5, of which 4 were waited for; matrix products, arithmetic and copies ran while one was open for 13% of the time, Pallas kernels for 0%

commit v1 on v0

--- a/solution.py
+++ b/solution.py
@@ -1,9 +1,396 @@
+import functools
+
 import jax
 import jax.numpy as jnp
 from jax import lax
+from jax.experimental import pallas as pl
+from jax.experimental.pallas import tpu as pltpu
 from jax.sharding import PartitionSpec as P
 
 step_rate = 0.3
+bf16 = jnp.bfloat16
+f32 = jnp.float32
+i32 = jnp.int32
+LANES = 128
+VMEM = pl.BlockSpec(memory_space=pltpu.VMEM)
+SMEM = pl.BlockSpec(memory_space=pltpu.SMEM)
+ANY = pl.BlockSpec(memory_space=pl.ANY)
+NN = (((1,), (0,)), ((), ()))
+NT = (((1,), (1,)), ((), ()))
+TN = (((0,), (0,)), ((), ()))
+
+
+def mm(a, b, dims=NN):
+    return lax.dot_general(a, b, dims, preferred_element_type=f32)
+
+
+def iota(shape, axis):
+    return lax.broadcasted_iota(i32, shape, axis)
+
+
+def onehot(flags):
+    return flags.astype(f32).astype(bf16)
+
+
+def halves_swapped(values):
+    return pltpu.roll(values, LANES // 2, 1)
+
+
+def request_kernel(
+    row_count, owner_count, capacity, neg_own,
+    head_ref, tail_ref, neg_ref, slot_ref, emb_ref,
+    pay_ref, place_ref, neg_row_ref, table_ref,
+    emb_buf, neg_buf, sems,
+):
+    feature_count = emb_ref.shape[0]
+    chunk = feature_count // 2
+    copies = [
+        pltpu.make_async_copy(
+            emb_ref.at[pl.ds(c * chunk, chunk)], emb_buf.at[pl.ds(c * chunk, chunk)], sems.at[c]
+        )
+        for c in range(2)
+    ]
+    for copy in copies:
+        copy.start()
+    slots = slot_ref[...]
+    slots_low = (slots & 255).astype(f32).astype(bf16)
+    slots_high = (slots >> 8).astype(f32).astype(bf16)
+
+    def lookup(ids):
+        count = ids.shape[1]
+        picks = onehot(iota((slots.shape[0], count), 0) == (ids >> 7))
+        columns = mm(slots_low, picks, TN) + 256.0 * mm(slots_high, picks, TN)
+        lane_of = iota((LANES, count), 0) == (ids & 127)
+        return jnp.sum(jnp.where(lane_of, columns, 0.0), axis=0, keepdims=True).astype(i32)
+
+    ids = jnp.concatenate([head_ref[...], tail_ref[...]], axis=1)
+    end_count = ids.shape[1]
+    end_slots = lookup(ids)
+    owner_of = end_slots // row_count
+    local_row = end_slots - owner_of * row_count + 1
+    owners = iota((owner_count, end_count), 0) == owner_of
+    earlier = onehot(iota((end_count, end_count), 0) < iota((end_count, end_count), 1))
+    before = mm(onehot(owners), earlier)
+    rank = jnp.sum(jnp.where(owners, before, 0.0), axis=0, keepdims=True).astype(i32)
+    place_ref[...] = owner_of * capacity + rank
+    low = jnp.where(owners, (local_row & 255).astype(f32), 0.0).astype(bf16)
+    high = jnp.where(owners, (local_row >> 8).astype(f32), 0.0).astype(bf16)
+    lane = iota((LANES, end_count), 0)
+    requests = mm(low, onehot(lane == rank), NT) + mm(high, onehot(lane == rank + capacity), NT)
+
+    lane_row = iota((1, LANES), 1)
+    neg_ids = jnp.zeros((1, LANES), i32)
+    for n in range(neg_own):
+        neg_ids = jnp.where(lane_row % neg_own == n, neg_ref[n], neg_ids)
+    neg_row = lookup(neg_ids)
+    neg_row = neg_row - (neg_row // row_count) * row_count
+    neg_row_ref[...] = neg_row
+    for copy in copies:
+        copy.wait()
+    table_ref[...] = emb_buf[...].astype(bf16)
+    neg_buf[...] = mm(table_ref[...], onehot(iota((row_count, LANES), 0) == neg_row))
+    groups = LANES // neg_own
+    piece = feature_count // groups
+    packed = jnp.zeros((piece, LANES), f32)
+    for g in range(groups):
+        packed = jnp.where(lane_row // neg_own == g, neg_buf[pl.ds(g * piece, piece), :], packed)
+    neg_buf[pl.ds(0, piece), :] = packed
+    neg_buf[pl.ds(piece, 8), :] = jnp.zeros((8, LANES), f32)
+    whole = piece // 16 * 16
+    main = neg_buf[pl.ds(0, whole), :].astype(bf16)
+    rest_rows = pay_ref.shape[1] - whole
+    rest = neg_buf[pl.ds(whole, rest_rows), :]
+    is_request = iota((rest_rows, LANES), 0) == piece - whole
+    for d in range(owner_count):
+        pay_ref[d, 0:whole, :] = main
+        pay_ref[d, whole : whole + rest_rows, :] = jnp.where(
+            is_request, requests[d : d + 1, :], rest
+        ).astype(bf16)
+
+
+def asked_lanes(req, owner_count):
+    value = req + 256.0 * halves_swapped(req)
+    other = halves_swapped(value)
+    left = iota((1, LANES), 1) < LANES // 2
+    rows = [
+        jnp.where(left, value[s : s + 1, :], other[s + 1 : s + 2, :])
+        for s in range(0, owner_count, 2)
+    ]
+    return jnp.concatenate(rows, axis=1).astype(i32)
+
+
+def pack_pair(values):
+    half = values.shape[0] // 2
+    real, imag = values[:half], values[half:]
+    left = iota((half, LANES), 1) < LANES // 2
+    first = jnp.where(left, real, halves_swapped(imag))
+    second = jnp.where(left, halves_swapped(real), imag)
+    return first.astype(bf16), second.astype(bf16)
+
+
+def unpack_pair(first, second):
+    first, second = first.astype(f32), second.astype(f32)
+    left = iota(first.shape, 1) < LANES // 2
+    real = jnp.where(left, first, halves_swapped(second))
+    imag = jnp.where(left, halves_swapped(first), second)
+    return real.astype(bf16), imag.astype(bf16)
+
+
+def answer_kernel(owner_count, req_row, got_ref, table_ref, out_ref, asked_ref):
+    row_count = table_ref.shape[1]
+    asked = asked_lanes(got_ref[:, req_row, :].astype(f32), owner_count)
+    asked_ref[...] = asked
+    width = 2 * LANES
+    for c in range(asked.shape[1] // width):
+        row = asked[:, c * width : (c + 1) * width]
+        picks = onehot(iota((row_count, width), 0) + 1 == row)
+        rows = mm(table_ref[...], picks)
+        for p in range(2):
+            first, second = pack_pair(rows[:, p * LANES : (p + 1) * LANES])
+            out_ref[4 * c + 2 * p] = first
+            out_ref[4 * c + 2 * p + 1] = second
+
+
+def relation_kernel(ids_ref, relations_ref, out_ref):
+    count = relations_ref.shape[1]
+    picks = onehot(iota((count, ids_ref.shape[1]), 0) == ids_ref[...])
+    out_ref[...] = mm(relations_ref[...], picks).astype(bf16)
+
+
+def edge_kernel(owner_count, got_ref, rel_ref, neg_ref, place_ref, out_ref, rows_buf):
+    half = got_ref.shape[1]
+    slot_count = rows_buf.shape[1]
+    end_count = place_ref.shape[1]
+    edge_count = end_count // 2
+    for s in range(0, owner_count, 2):
+        real, imag = unpack_pair(got_ref[s], got_ref[s + 1])
+        lanes = pl.ds(s // 2 * LANES, LANES)
+        rows_buf[0:half, lanes] = real.astype(f32)
+        rows_buf[half : 2 * half, lanes] = imag.astype(f32)
+    places = onehot(iota((slot_count, end_count), 0) == place_ref[...])
+    ends = mm(rows_buf[...].astype(bf16), places)
+    head_re, head_im = ends[:half, :edge_count], ends[half:, :edge_count]
+    tail_re, tail_im = ends[:half, edge_count:], ends[half:, edge_count:]
+    rel = rel_ref[...].astype(f32)
+    rel_re, rel_im = rel[:half], rel[half:]
+    neg = neg_ref[...]
+    neg_count = neg.shape[0]
+    product_re = head_re * rel_re - head_im * rel_im
+    product_im = head_re * rel_im + head_im * rel_re
+    product_low = jnp.concatenate([product_re, product_im], axis=0).astype(bf16)
+    mirror_low = jnp.concatenate(
+        [rel_re * tail_re + rel_im * tail_im, rel_re * tail_im - rel_im * tail_re], axis=0
+    ).astype(bf16)
+    positive = jnp.sum(product_re * tail_re + product_im * tail_im, axis=0, keepdims=True)
+    pos_grad = -jax.nn.sigmoid(-positive)
+    tail_weight = (jax.nn.sigmoid(mm(neg, product_low)) / neg_count).astype(bf16)
+    head_weight = (jax.nn.sigmoid(mm(neg, mirror_low)) / neg_count).astype(bf16)
+    neg_grad = mm(tail_weight, product_low, NT) + mm(head_weight, mirror_low, NT)
+    own = neg_count // owner_count
+    tiles = (2 * half + LANES - 1) // LANES
+    neg_low = neg_grad.astype(bf16)
+    for t in range(tiles):
+        width = min(LANES, 2 * half - t * LANES)
+        for d in range(owner_count):
+            out_ref[d, t * own : (t + 1) * own, 0:width] = neg_low[
+                d * own : (d + 1) * own, t * LANES : t * LANES + width
+            ]
+    grad = mm(neg, tail_weight, TN)
+    back = mm(neg, head_weight, TN)
+    grad_re = grad[:half] + pos_grad * tail_re
+    grad_im = grad[half:] + pos_grad * tail_im
+    back_re, back_im = back[:half], back[half:]
+    head_grad = jnp.concatenate(
+        [grad_re * rel_re + grad_im * rel_im, grad_im * rel_re - grad_re * rel_im], axis=0
+    ).astype(bf16)
+    tail_grad = jnp.concatenate(
+        [
+            pos_grad * product_re + (back_re * rel_re - back_im * rel_im),
+            pos_grad * product_im + (back_re * rel_im + back_im * rel_re),
+        ],
+        axis=0,
+    ).astype(bf16)
+    grads = jnp.concatenate([head_grad, tail_grad], axis=1)
+    base = tiles * own
+    width = 2 * LANES
+    for c in range(slot_count // width):
+        sent = mm(grads, places[c * width : (c + 1) * width, :], NT)
+        for p in range(2):
+            first, second = pack_pair(sent[:, p * LANES : (p + 1) * LANES])
+            out_ref[4 * c + 2 * p, base : base + half, :] = first
+            out_ref[4 * c + 2 * p + 1, base : base + half, :] = second
+
+
+def gather_grads(owner_count, base, got_ref, buf):
+    half = got_ref.shape[1] - base
+    own = base // 4
+    slot_count = owner_count * LANES // 2
+    for s in range(0, owner_count, 2):
+        real, imag = unpack_pair(got_ref[s, base:, :], got_ref[s + 1, base:, :])
+        lanes = pl.ds(s // 2 * LANES, LANES)
+        buf[0:half, lanes] = real
+        buf[half : 2 * half, lanes] = imag
+    total = got_ref[0, 0:base, :].astype(f32)
+    for s in range(1, owner_count):
+        total = total + got_ref[s, 0:base, :].astype(f32)
+    parts = [total[t * own : (t + 1) * own].T for t in range(4)]
+    neg = jnp.concatenate(parts, axis=0)[: 2 * half]
+    high = neg.astype(bf16)
+    buf[0 : 2 * half, slot_count : slot_count + own] = high
+    buf[0 : 2 * half, slot_count + own : slot_count + 2 * own] = (neg - high.astype(f32)).astype(bf16)
+
+
+def sum_kernel(owner_count, base, own, got_ref, asked_ref, neg_row_ref, out_ref, buf):
+    @pl.when(pl.program_id(0) == 0)
+    def _():
+        gather_grads(owner_count, base, got_ref, buf)
+
+    out_ref[...] = block_sum(own, asked_ref, neg_row_ref, buf, out_ref.shape[1])
+
+
+def block_sum(own, asked_ref, neg_row_ref, buf, rows):
+    first = pl.program_id(0) * rows
+    asked = jnp.concatenate([asked_ref[...], neg_row_ref[:, 0 : 2 * own] + 1], axis=1)
+    targets = onehot(iota((rows, asked.shape[1]), 0) + first + 1 == asked)
+    return mm(buf[...], targets, NT)
+
+
+def update_kernel(
+    owner_count, base, own,
+    got_ref, asked_ref, neg_row_ref, mine_ref, emb_ref, acc_ref, new_ref, state_ref, buf,
+):
+    @pl.when(pl.program_id(0) == 0)
+    def _():
+        gather_grads(owner_count, base, got_ref, buf)
+
+    grad = mine_ref[...] + block_sum(own, asked_ref, neg_row_ref, buf, new_ref.shape[1])
+    state = acc_ref[...] + jnp.sum(grad * grad, axis=0, keepdims=True) / grad.shape[0]
+    state_ref[...] = state
+    new_ref[...] = emb_ref[...] - grad * (step_rate / jnp.sqrt(state))
+
+
+def call(kernel, outs, in_specs, scratch=(), limit=40 << 20, cost=None, **grid):
+    return pl.pallas_call(
+        kernel,
+        out_shape=outs,
+        in_specs=in_specs,
+        scratch_shapes=list(scratch),
+        compiler_params=pltpu.CompilerParams(vmem_limit_bytes=limit),
+        cost_estimate=cost,
+        **grid,
+    )
+
+
+def cost(flops, moved):
+    return pl.CostEstimate(flops=flops, bytes_accessed=moved, transcendentals=0)
+
+
+def exchange(values):
+    return lax.all_to_all(values, "ent", split_axis=0, concat_axis=0, tiled=True)
+
+
+def packed_shards(
+    head_ids, rel_ids, tail_ids, neg_ids, slot_of, relations, embeddings, accumulator
+):
+    row_count, features = embeddings.shape
+    half = features // 2
+    owners = lax.axis_size("ent")
+    edges = head_ids.shape[0]
+    ends = 2 * edges
+    capacity = 2 * ends // owners
+    slots = owners * capacity
+    own = neg_ids.shape[0]
+    table = embeddings.T
+    shape = jax.ShapeDtypeStruct
+    groups = LANES // own
+    piece = features // groups
+    pay_rows = (piece + 1 + 7) // 8 * 8
+
+    payload, place, neg_row, low_table = call(
+        functools.partial(request_kernel, row_count, owners, capacity, own),
+        (
+            shape((owners, pay_rows, LANES), bf16),
+            shape((1, ends), i32),
+            shape((1, LANES), i32),
+            shape((features, row_count), bf16),
+        ),
+        [VMEM, VMEM, SMEM, VMEM, ANY],
+        [
+            pltpu.VMEM((features, row_count), f32),
+            pltpu.VMEM((features, LANES), f32),
+            pltpu.SemaphoreType.DMA((2,)),
+        ],
+        limit=20 << 20,
+    )(
+        head_ids.reshape(1, edges),
+        tail_ids.reshape(1, edges),
+        neg_ids,
+        slot_of.reshape(-1, LANES),
+        table,
+    )
+    got = exchange(payload)
+    answers, asked = call(
+        functools.partial(answer_kernel, owners, piece),
+        (shape((owners, half, LANES), bf16), shape((1, slots), i32)),
+        [VMEM] * 2,
+        limit=20 << 20,
+    )(got, low_table)
+    fetched = exchange(answers)
+    neg_rows = (
+        got[:, :piece, :]
+        .reshape(owners, piece, groups, own)
+        .transpose(0, 3, 2, 1)
+        .reshape(owners * own, features)
+    )
+    rel_rows = call(
+        relation_kernel,
+        shape((features, edges), bf16),
+        [VMEM] * 2,
+        limit=20 << 20,
+        cost=cost(2 * features * relations.shape[0] * edges, relations.size * 2),
+    )(rel_ids.reshape(1, edges), relations.T)
+    other_asked = lax.ppermute(asked, "rep", [(0, 1), (1, 0)])
+    base = 4 * own
+    outgoing = call(
+        functools.partial(edge_kernel, owners),
+        shape((owners, base + half, LANES), bf16),
+        [VMEM] * 4,
+        [pltpu.VMEM((features, slots), f32)],
+        limit=30 << 20,
+    )(fetched, rel_rows, neg_rows, place)
+    incoming = exchange(outgoing)
+    other = lax.ppermute(incoming, "rep", [(0, 1), (1, 0)])
+    block = 256
+    columns = lambda i: (0, i)
+    fixed = lambda rank: (lambda i: (0,) * rank)
+    got_specs = [
+        pl.BlockSpec((owners, base + half, LANES), fixed(3)),
+        pl.BlockSpec((1, slots), fixed(2)),
+        pl.BlockSpec((1, LANES), fixed(2)),
+    ]
+    wide = pl.BlockSpec((features, block), columns)
+    thin = pl.BlockSpec((1, block), columns)
+    buf = pltpu.VMEM((features, slots + 2 * own), bf16)
+    mine = call(
+        functools.partial(sum_kernel, owners, base, own),
+        shape((features, row_count), f32),
+        got_specs,
+        [buf],
+        limit=20 << 20,
+        cost=cost(2 * features * slots * row_count, 4 * features * row_count),
+        grid=(row_count // block,),
+        out_specs=wide,
+    )(incoming, asked, neg_row)
+    new_rows, new_state = call(
+        functools.partial(update_kernel, owners, base, own),
+        (shape((features, row_count), f32), shape((1, row_count), f32)),
+        got_specs + [wide, wide, thin],
+        [buf],
+        limit=20 << 20,
+        grid=(row_count // block,),
+        out_specs=(wide, thin),
+    )(other, other_asked, neg_row, mine, table, accumulator.reshape(1, row_count))
+    return new_rows.T, new_state.reshape(row_count)
 
 
 def split_parts(values):
@@ -132,6 +519,32 @@
     return (new_rows, new_state)
 
 
+def fits_packed(mesh, features, rows, edges, negs, entities):
+    owners = mesh.shape["ent"]
+    return (
+        4 * edges == owners * LANES // 2
+        and mesh.shape["rep"] == 2
+        and owners % 4 == 0
+        and LANES % negs == 0
+        and features % 16 == 0
+        and features <= 4 * LANES
+        and 3 * LANES < features
+        and features % (LANES // negs) == 0
+        and rows % 256 == 0
+        and rows < 256 * 255
+        and entities % LANES == 0
+        and entities <= 1 << 16
+    )
+
+
+def any_shards(mesh, *arrays):
+    head_ids, _, _, neg_ids, slot_of, _, embeddings, _ = arrays
+    rows, features = embeddings.shape
+    if fits_packed(mesh, features, rows, head_ids.shape[0], neg_ids.shape[0], slot_of.shape[0]):
+        return packed_shards(*arrays)
+    return shards(*arrays)
+
+
 def solution(mesh):
     placed = (
         P(("ent", "rep")),
@@ -144,5 +557,5 @@
         P("ent"),
     )
     return jax.shard_map(
-        shards, mesh=mesh, in_specs=placed, out_specs=(P("ent", None), P("ent")), check_vma=False
-    )
+        functools.partial(any_shards, mesh), mesh=mesh, in_specs=placed, out_specs=(P("ent", None), P("ent")), check_vma=False
+    )

time: 263 us -> 100 us (0.38)
  waiting for transfers between devices: 93.1 us -> 16.5 us
  other arithmetic: 41.9 us -> 0 us
  local copies, waits for them, and re-layouts: 49.5 us -> 8.15 us
  Pallas kernels: 0 us -> 20.1 us
  between operations: 14.5 us -> 0.77 us
  starting transfers between devices: 17.7 us -> 4.81 us
  blocking collectives: 42.7 us -> 49.3 us
    all_to_all x0 -> x2, blocking collectives: none -> 49.3 us  [exchange(): lax.all_to_all(values, 'ent', split_axis=0, concat_axis=0, tiled=True)]
    all_gather x1 -> x0, blocking collectives: 42.7 us -> none  [shards(): neg_rows = lax.all_gather(own_negs, 'ent', axis=0, tiled=True)]
    reduce_scatter x1 -> x0, waiting for transfers between devices: 29.7 us -> none  [shards(): lax.psum_scatter(neg_grad, 'ent', scatter_dimension=0, tiled=True)]
    psum x1 -> x0, waiting for transfers between devices: 24.6 us -> none  [shards(): summed = lax.psum(partial_sum, 'rep')]
    all_to_all x3 -> x1, waiting for transfers between devices: 38.8 us -> 16.5 us  [exchange(): lax.all_to_all(values, 'ent', split_axis=0, concat_axis=0, tiled=True)]
    pallas_call x0 -> x6, Pallas kernels: none -> 20.1 us  [the longest x1 6.73 us: packed_shards(): call(functools.partial(update_kernel, owners, base, own), (shape((feature...]
    gather x9 -> x0, local copies, waits for them, and re-layouts: 18.6 us -> none  [the longest x2 4.07 us: shards(): rel_rows = relations[rel_ids]]
    scatter-add x2 -> x0, other arithmetic: 13.8 us -> none  [the longest x1 8.75 us: shards(): jax.ops.segment_sum(incoming, targets, num_segments=row_count + 1)]
  transfers between devices with their start and end apart: 5 -> 3, of which waited for: 4 -> 1; matrix products, arithmetic and copies ran while one was open for 13% -> 1% of each run, Pallas kernels for 0% -> 6%
where the time goes in v1:
time: 100 us; the launch traced here: 99.6 us
  blocking collectives  49.3 us (49%)
  Pallas kernels  20.1 us (20%)
  waiting for transfers between devices  16.5 us (16%)
  local copies, waits for them, and re-layouts  8.15 us (8%)
  starting transfers between devices  4.81 us (5%)
    all_to_all x2, blocking collectives, exchange(): lax.all_to_all(values, 'ent', split_axis=0, concat_axis=0, tiled=True)  49.3 us
    all_to_all x1, waiting for transfers between devices, exchange(): lax.all_to_all(values, 'ent', split_axis=0, concat_axis=0, tiled=True)  16.5 us
    unnamed x24, local copies, waits for them, and re-layouts  7.34 us
    pallas_call x1, Pallas kernels, packed_shards(): call(functools.partial(update_kernel, owners, base, own), (shape((feature...  6.73 us
    pallas_call x1, Pallas kernels, packed_shards(): call(functools.partial(sum_kernel, owners, base, own), shape((features, r...  4.57 us
    all_to_all x1, starting transfers between devices, exchange(): lax.all_to_all(values, 'ent', split_axis=0, concat_axis=0, tiled=True)  4.3 us
    pallas_call x1, Pallas kernels, packed_shards(): call(functools.partial(edge_kernel, owners), shape((owners, base + half,...  3.33 us
    pallas_call x1, Pallas kernels, packed_shards(): call(functools.partial(request_kernel, row_count, owners, capacity, own),...  2.31 us
  transfers between devices with their start and end apart: 3, of which 1 were waited for; matrix products, arithmetic and copies ran while one was open for 1% of the time, Pallas kernels for 6%

profile of v1, /device:TPU:0, one launch (start us, length us, event | category | flops | bytes accessed | tf_op | source)
XLA Modules:
  0.0 99.6 jit_solution(7738031830923376208)
XLA Ops:
  0.6 0.0 copy-start
  0.6 1.9 %copy-done = f32[2048,400]{0,1:T(8,128)S(1)} copy-done((f32[2048,400]{0,1:T(8,128)S(1)}, f32[2048,400]{0,1:T(8,128)}, u32[]{:S(2)}) %copy-start) | copy-done | bytes 3276824
  2.6 0.0 copy-start.6
  2.6 0.9 copy-done.6
  3.5 0.0 copy-start.8
  3.5 0.7 copy-done.8
  4.1 0.0 copy-start.9
  4.1 0.7 copy-done.9
  4.8 0.0 copy-start.11
  4.8 0.7 copy-done.11
  5.5 0.0 copy-start.2
  5.5 0.0 copy-start.10
  5.5 2.3 %shard_map.95 = (bf16[16,56,128]{2,1,0:T(8,128)(2,1)S(1)}, s32[1,512]{1,0:T(1,128)S(1)}, s32[1,128]{1,0:T(1,128)S(1)}, bf16[400,2048]{1,0:T(8,128)(2,1)S(1)}) custom-call(s32[1,256]{1,0:T(1,128)S(1)} %bitcast.21, s32[1,256]{1,0:T(1,128)S(1)} %bitcast.22, s32[16]{0:T(128)S(1)} %copy-done.11, s32[256,128]{1,0:T(8,128)S(1)} %bitcast.19, f32[400,2048]{1,0:T(8,128)S(1)} %bitcast.15), custom_call_target="tpu_custom_call" | custom-call | tf_op jit(solution)/shard_map/pallas_call | solution.py:309
  7.8 17.4 %all_to_all.15.got_ref = bf16[16,56,128]{2,1,0:T(8,128)(2,1)S(1)} all-to-all(bf16[16,56,128]{2,1,0:T(8,128)(2,1)S(1)} %get-tuple-element.10), channel_id=1, replica_groups=mesh['ent'=16,'rep'=2] {'ent'}, dimensions={0} | all-to-all | bytes 458752 | tf_op jit(solution)/shard_map/all_to_all | solution.py:289
  25.2 2.1 %shard_map.96 = (bf16[16,200,128]{2,1,0:T(8,128)(2,1)S(1)}, s32[1,1024]{1,0:T(1,128)S(1)}) custom-call(bf16[16,56,128]{2,1,0:T(8,128)(2,1)S(1)} %all_to_all.15.got_ref, bf16[400,2048]{1,0:T(8,128)(2,1)S(1)} %get-tuple-element.11.table_ref), custom_call_target="tpu_custom_call" | custom-call | tf_op jit(solution)/shard_map/pallas_call | solution.py:332
  27.3 0.0 copy-start.3
  27.3 0.9 copy-done.3
  28.2 4.3 %all-to-all-start.1 = ((bf16[16,200,128]{2,1,0:T(8,128)(2,1)}), bf16[16,200,128]{2,1,0:T(8,128)(2,1)}, u32[]{:S(2)}, u32[]{:S(2)}) async-start(bf16[16,200,128]{2,1,0:T(8,128)(2,1)} %copy-done.3), calls=%async_computation.1 | async-start | bytes 1638400 | tf_op jit(solution)/shard_map/all_to_all | solution.py:289
  32.5 0.0 copy-done.2
  32.5 0.0 copy-done.10
  32.5 1.0 %shard_map.97.rel_ref = bf16[400,256]{1,0:T(8,128)(2,1)S(1)} custom-call(s32[1,256]{1,0:T(1,128)S(1)} %bitcast.23, bf16[400,4096]{1,0:T(8,128)(2,1)S(1)} %bitcast.17), custom_call_target="tpu_custom_call" | custom-call | flops 838860800 | bytes 3276800 | tf_op jit(solution)/shard_map/pallas_call | solution.py:345
  33.5 0.0 copy-start.4
  33.6 0.7 copy-done.4
  34.2 0.3 copy.11
  34.5 0.1 copy.12
  34.7 0.4 reshape.33.neg_ref
  35.1 16.5 %all-to-all-done.1.got_ref = bf16[16,200,128]{2,1,0:T(8,128)(2,1)} async-done(((bf16[16,200,128]{2,1,0:T(8,128)(2,1)}), bf16[16,200,128]{2,1,0:T(8,128)(2,1)}, u32[]{:S(2)}, u32[]{:S(2)}) %all-to-all-start.1) | async-done | bytes 819232 | tf_op jit(solution)/shard_map/all_to_all | solution.py:289
  51.5 0.0 copy-start.5
  51.5 0.9 copy-done.5
  52.5 3.3 %shard_map.98 = bf16[16,264,128]{2,1,0:T(8,128)(2,1)S(1)} custom-call(bf16[16,200,128]{2,1,0:T(8,128)(2,1)} %all-to-all-done.1.got_ref, bf16[400,256]{1,0:T(8,128)(2,1)S(1)} %copy-done.5, bf16[256,400]{1,0:T(8,128)(2,1)S(1)} %reshape.33.neg_ref, s32[1,512]{1,0:T(1,128)S(1)} %get-tuple-element.13.place_ref), custom_call_target="tpu_custom_call" | custom-call | tf_op jit(solution)/shard_map/pallas_call | solution.py:354
  55.8 31.9 %all_to_all.16.got_ref = bf16[16,264,128]{2,1,0:T(8,128)(2,1)S(1)} all-to-all(bf16[16,264,128]{2,1,0:T(8,128)(2,1)S(1)} %shard_map.98), channel_id=1, replica_groups=mesh['ent'=16,'rep'=2] {'ent'}, dimensions={0} | all-to-all | bytes 2162688 | tf_op jit(solution)/shard_map/all_to_all | solution.py:289
  87.7 0.0 copy-start.1
  87.7 0.0 copy-start.7
  87.7 0.0 collective-permute-start
  87.7 0.5 collective-permute-start.1
  88.2 4.6 %shard_map.99.mine_ref = f32[400,2048]{1,0:T(8,128)S(1)} custom-call(bf16[16,264,128]{2,1,0:T(8,128)(2,1)S(1)} %all_to_all.16.got_ref, s32[1,1024]{1,0:T(1,128)S(1)} %get-tuple-element.14.asked_ref, s32[1,128]{1,0:T(1,128)S(1)} %get-tuple-element.15.neg_row_ref), custom_call_target="tpu_custom_call" | custom-call | flops 1677721600 | bytes 3276800 | tf_op jit(solution)/shard_map/pallas_call | solution.py:374
  92.8 0.0 collective-permute-done.1.asked_ref
  92.8 0.0 collective-permute-done.got_ref
  92.8 0.0 copy-done.1
  92.8 0.0 copy-done.7
  92.8 6.7 %shard_map.100 = (f32[400,2048]{1,0:T(8,128)}, f32[1,2048]{1,0:T(1,128)}) custom-call(bf16[16,264,128]{2,1,0:T(8,128)(2,1)S(1)} %collective-permute-done.got_ref, s32[1,1024]{1,0:T(1,128)S(1)} %collective-permute-done.1.asked_ref, s32[1,128]{1,0:T(1,128)S(1)} %get-tuple-element.15.neg_row_ref, f32[400,2048]{1,0:T(8,128)S(1)} %shard_map.99.mine_ref, ...), custom_call_target="tpu_custom_call" | custom-call | tf_op jit(solution)/shard_map/pallas_call | solution.py:384
Async XLA Ops:
  0.6 1.9 %copy-start = (f32[2048,400]{0,1:T(8,128)S(1)}, f32[2048,400]{0,1:T(8,128)}, u32[]{:S(2)}) copy-start(f32[2048,400]{0,1:T(8,128)} %param.14) | copy-start | bytes 9830404
  2.6 0.9 copy-start.6
  3.5 0.7 copy-start.8
  4.1 0.7 copy-start.9
  4.8 0.7 copy-start.11
  5.5 27.0 %copy-start.2 = (bf16[4096,400]{0,1:T(8,128)(2,1)S(1)}, bf16[4096,400]{0,1:T(8,128)(2,1)}, u32[]{:S(2)}) copy-start(bf16[4096,400]{0,1:T(8,128)(2,1)} %param.13) | copy-start | bytes 9830404
  5.5 27.0 %copy-start.10 = (s32[256]{0:T(256)S(1)}, s32[256]{0:T(256)}, u32[]{:S(2)}) copy-start(s32[256]{0:T(256)} %param.9) | copy-start | bytes 3076
  27.3 0.9 copy-start.3
  28.2 23.3 %all-to-all-start.1 = ((bf16[16,200,128]{2,1,0:T(8,128)(2,1)}), bf16[16,200,128]{2,1,0:T(8,128)(2,1)}, u32[]{:S(2)}, u32[]{:S(2)}) async-start(bf16[16,200,128]{2,1,0:T(8,128)(2,1)} %copy-done.3), calls=%async_computation.1 | async-start | bytes 1638400 | tf_op jit(solution)/shard_map/all_to_all | solution.py:289
  33.5 0.7 copy-start.4
  51.5 0.9 copy-start.5
  87.7 5.1 %copy-start.1 = (f32[2048,400]{0,1:T(8,128)S(1)}, f32[2048,400]{0,1:T(8,128)}, u32[]{:S(2)}) copy-start(f32[2048,400]{0,1:T(8,128)} %param.14) | copy-start | bytes 9830404
  87.7 5.1 %copy-start.7 = (f32[2048]{0:T(1024)S(1)}, f32[2048]{0:T(1024)}, u32[]{:S(2)}) copy-start(f32[2048]{0:T(1024)} %param.15) | copy-start | bytes 24580
  87.7 5.1 %collective-permute-start = (bf16[16,264,128]{2,1,0:T(8,128)(2,1)S(1)}, bf16[16,264,128]{2,1,0:T(8,128)(2,1)S(1)}, u32[]{:S(2)}, u32[]{:S(2)}) collective-permute-start(bf16[16,264,128]{2,1,0:T(8,128)(2,1)S(1)} %all_to_all.16.got_ref), channel_id=1, source_target_pairs={{0,1},{1,0},{2,3},{3,2},{4,5},{5,4},{6,7},{7,6},{8,9},{9,8},{10,11... | collective-permute-start | bytes 3244040 | tf_op jit(solution)/shard_map/ppermute | solution.py:362
  87.7 5.1 %collective-permute-start.1 = (s32[1,1024]{1,0:T(1,128)S(1)}, s32[1,1024]{1,0:T(1,128)S(1)}, u32[]{:S(2)}, u32[]{:S(2)}) collective-permute-start(s32[1,1024]{1,0:T(1,128)S(1)} %get-tuple-element.14.asked_ref), channel_id=1, source_target_pairs={{0,1},{1,0},{2,3},{3,2},{4,5},{5,4},{6,7},{7,6},{8,9},{9,8},{10,11... | collective-permute-start | bytes 12296 | tf_op jit(solution)/shard_map/ppermute | solution.py:352

commit v2 on v1

--- a/solution.py
+++ b/solution.py
@@ -13,8 +13,7 @@
 i32 = jnp.int32
 LANES = 128
 VMEM = pl.BlockSpec(memory_space=pltpu.VMEM)
-SMEM = pl.BlockSpec(memory_space=pltpu.SMEM)
-ANY = pl.BlockSpec(memory_space=pl.ANY)
+HBM = pl.BlockSpec(memory_space=pltpu.HBM)
 NN = (((1,), (0,)), ((), ()))
 NT = (((1,), (1,)), ((), ()))
 TN = (((0,), (0,)), ((), ()))
@@ -38,20 +37,29 @@
 
 def request_kernel(
     row_count, owner_count, capacity, neg_own,
-    head_ref, tail_ref, neg_ref, slot_ref, emb_ref,
+    head_hbm, tail_hbm, neg_hbm, slot_hbm, emb_hbm,
     pay_ref, place_ref, neg_row_ref, table_ref,
-    emb_buf, neg_buf, sems,
+    ids_ref, neg_ref, slot_ref, emb_buf, neg_buf, sems,
 ):
-    feature_count = emb_ref.shape[0]
+    edge_count = head_hbm.shape[1]
+    feature_count = emb_hbm.shape[0]
     chunk = feature_count // 2
+    small = [
+        pltpu.make_async_copy(head_hbm, ids_ref.at[:, pl.ds(0, edge_count)], sems.at[0]),
+        pltpu.make_async_copy(tail_hbm, ids_ref.at[:, pl.ds(edge_count, edge_count)], sems.at[1]),
+        pltpu.make_async_copy(neg_hbm, neg_ref, sems.at[2]),
+        pltpu.make_async_copy(slot_hbm, slot_ref, sems.at[3]),
+    ]
     copies = [
         pltpu.make_async_copy(
-            emb_ref.at[pl.ds(c * chunk, chunk)], emb_buf.at[pl.ds(c * chunk, chunk)], sems.at[c]
+            emb_hbm.at[pl.ds(c * chunk, chunk)], emb_buf.at[pl.ds(c * chunk, chunk)], sems.at[4 + c]
         )
         for c in range(2)
     ]
-    for copy in copies:
+    for copy in small + copies:
         copy.start()
+    for copy in small:
+        copy.wait()
     slots = slot_ref[...]
     slots_low = (slots & 255).astype(f32).astype(bf16)
     slots_high = (slots >> 8).astype(f32).astype(bf16)
@@ -63,7 +71,7 @@
         lane_of = iota((LANES, count), 0) == (ids & 127)
         return jnp.sum(jnp.where(lane_of, columns, 0.0), axis=0, keepdims=True).astype(i32)
 
-    ids = jnp.concatenate([head_ref[...], tail_ref[...]], axis=1)
+    ids = ids_ref[...]
     end_count = ids.shape[1]
     end_slots = lookup(ids)
     owner_of = end_slots // row_count
@@ -108,7 +116,35 @@
         ).astype(bf16)
 
 
-def asked_lanes(req, owner_count):
+def pack_pair(values):
+    half = values.shape[0] // 2
+    real, imag = values[:half], values[half:]
+    left = iota((half, LANES), 1) < LANES // 2
+    first = jnp.where(left, real, halves_swapped(imag))
+    second = jnp.where(left, halves_swapped(real), imag)
+    return first.astype(bf16), second.astype(bf16)
+
+
+def unpack_pair(first, second):
+    first, second = first.astype(f32), second.astype(f32)
+    left = iota(first.shape, 1) < LANES // 2
+    real = jnp.where(left, first, halves_swapped(second))
+    imag = jnp.where(left, halves_swapped(first), second)
+    return real.astype(bf16), imag.astype(bf16)
+
+
+def unpack_rows(got_ref, buf):
+    half = buf.shape[0] // 2
+    for s in range(0, got_ref.shape[0], 2):
+        real, imag = unpack_pair(got_ref[s, 0:half, :], got_ref[s + 1, 0:half, :])
+        lanes = pl.ds(s // 2 * LANES, LANES)
+        buf[0:half, lanes] = real
+        buf[half : 2 * half, lanes] = imag
+
+
+def answer_kernel(owner_count, req_row, got_ref, table_ref, out_hbm, asked_ref, out_buf, sems):
+    row_count = table_ref.shape[1]
+    req = got_ref[:, req_row, :].astype(f32)
     value = req + 256.0 * halves_swapped(req)
     other = halves_swapped(value)
     left = iota((1, LANES), 1) < LANES // 2
@@ -116,39 +152,23 @@
         jnp.where(left, value[s : s + 1, :], other[s + 1 : s + 2, :])
         for s in range(0, owner_count, 2)
     ]
-    return jnp.concatenate(rows, axis=1).astype(i32)
-
-
-def pack_pair(values):
-    half = values.shape[0] // 2
-    real, imag = values[:half], values[half:]
-    left = iota((half, LANES), 1) < LANES // 2
-    first = jnp.where(left, real, halves_swapped(imag))
-    second = jnp.where(left, halves_swapped(real), imag)
-    return first.astype(bf16), second.astype(bf16)
-
-
-def unpack_pair(first, second):
-    first, second = first.astype(f32), second.astype(f32)
-    left = iota(first.shape, 1) < LANES // 2
-    real = jnp.where(left, first, halves_swapped(second))
-    imag = jnp.where(left, halves_swapped(first), second)
-    return real.astype(bf16), imag.astype(bf16)
-
-
-def answer_kernel(owner_count, req_row, got_ref, table_ref, out_ref, asked_ref):
-    row_count = table_ref.shape[1]
-    asked = asked_lanes(got_ref[:, req_row, :].astype(f32), owner_count)
+    asked = jnp.concatenate(rows, axis=1).astype(i32)
     asked_ref[...] = asked
     width = 2 * LANES
+    copies = []
     for c in range(asked.shape[1] // width):
         row = asked[:, c * width : (c + 1) * width]
         picks = onehot(iota((row_count, width), 0) + 1 == row)
         rows = mm(table_ref[...], picks)
         for p in range(2):
             first, second = pack_pair(rows[:, p * LANES : (p + 1) * LANES])
-            out_ref[4 * c + 2 * p] = first
-            out_ref[4 * c + 2 * p + 1] = second
+            out_buf[4 * c + 2 * p] = first
+            out_buf[4 * c + 2 * p + 1] = second
+        part = pl.ds(4 * c, 4)
+        copies.append(pltpu.make_async_copy(out_buf.at[part], out_hbm.at[part], sems.at[c]))
+        copies[-1].start()
+    for copy in copies:
+        copy.wait()
 
 
 def relation_kernel(ids_ref, relations_ref, out_ref):
@@ -157,18 +177,48 @@
     out_ref[...] = mm(relations_ref[...], picks).astype(bf16)
 
 
-def edge_kernel(owner_count, got_ref, rel_ref, neg_ref, place_ref, out_ref, rows_buf):
-    half = got_ref.shape[1]
+def pack_neg_grad(neg_grad, out_buf, base):
+    owner_count = out_buf.shape[0]
+    own = neg_grad.shape[0] // owner_count
+    tiles = neg_grad.shape[1] // LANES
+    rest = neg_grad.shape[1] - tiles * LANES
+    last = jnp.concatenate(
+        [neg_grad[:, tiles * LANES :], jnp.zeros((neg_grad.shape[0], LANES - rest), f32)], axis=1
+    )
+    beside = pltpu.roll(last, rest, 1)
+    left = iota((own // 2, LANES), 1) < rest
+    for d in range(owner_count):
+        first, middle, end = d * own, d * own + own // 2, (d + 1) * own
+        parts = [neg_grad[first:end, t * LANES : (t + 1) * LANES] for t in range(tiles)]
+        parts.append(jnp.where(left, last[first:middle], beside[middle:end]))
+        packed = jnp.concatenate(parts, axis=0)
+        out_buf[d, base : base + packed.shape[0], :] = packed.astype(bf16)
+
+
+def neg_total(got_ref, features):
+    base = features // 2
+    total = got_ref[0, base:, :].astype(f32)
+    for s in range(1, got_ref.shape[0]):
+        total = total + got_ref[s, base:, :].astype(f32)
+    tiles = features // LANES
+    rest = features - tiles * LANES
+    own = total.shape[0] * 2 // (2 * tiles + 1)
+    last = total[tiles * own :]
+    last = jnp.concatenate([last, pltpu.roll(last, LANES - rest, 1)], axis=0)[:, :rest]
+    neg = jnp.concatenate([total[t * own : (t + 1) * own] for t in range(tiles)] + [last], axis=1)
+    high = neg.astype(bf16)
+    low = (neg - high.astype(f32)).astype(bf16)
+    return jnp.concatenate([high, low], axis=0)
+
+
+def edge_kernel(got_ref, rel_ref, neg_ref, place_ref, _, out_hbm, rows_buf, out_buf, sems):
+    owner_count, half, _ = got_ref.shape
     slot_count = rows_buf.shape[1]
     end_count = place_ref.shape[1]
     edge_count = end_count // 2
-    for s in range(0, owner_count, 2):
-        real, imag = unpack_pair(got_ref[s], got_ref[s + 1])
-        lanes = pl.ds(s // 2 * LANES, LANES)
-        rows_buf[0:half, lanes] = real.astype(f32)
-        rows_buf[half : 2 * half, lanes] = imag.astype(f32)
+    unpack_rows(got_ref, rows_buf)
     places = onehot(iota((slot_count, end_count), 0) == place_ref[...])
-    ends = mm(rows_buf[...].astype(bf16), places)
+    ends = mm(rows_buf[...], places)
     head_re, head_im = ends[:half, :edge_count], ends[half:, :edge_count]
     tail_re, tail_im = ends[:half, edge_count:], ends[half:, edge_count:]
     rel = rel_ref[...].astype(f32)
@@ -185,16 +235,6 @@
     pos_grad = -jax.nn.sigmoid(-positive)
     tail_weight = (jax.nn.sigmoid(mm(neg, product_low)) / neg_count).astype(bf16)
     head_weight = (jax.nn.sigmoid(mm(neg, mirror_low)) / neg_count).astype(bf16)
-    neg_grad = mm(tail_weight, product_low, NT) + mm(head_weight, mirror_low, NT)
-    own = neg_count // owner_count
-    tiles = (2 * half + LANES - 1) // LANES
-    neg_low = neg_grad.astype(bf16)
-    for t in range(tiles):
-        width = min(LANES, 2 * half - t * LANES)
-        for d in range(owner_count):
-            out_ref[d, t * own : (t + 1) * own, 0:width] = neg_low[
-                d * own : (d + 1) * own, t * LANES : t * LANES + width
-            ]
     grad = mm(neg, tail_weight, TN)
     back = mm(neg, head_weight, TN)
     grad_re = grad[:half] + pos_grad * tail_re
@@ -211,82 +251,92 @@
         axis=0,
     ).astype(bf16)
     grads = jnp.concatenate([head_grad, tail_grad], axis=1)
-    base = tiles * own
+    neg_grad = mm(tail_weight, product_low, NT) + mm(head_weight, mirror_low, NT)
+    pack_neg_grad(neg_grad, out_buf, half)
     width = 2 * LANES
+    copies = []
     for c in range(slot_count // width):
         sent = mm(grads, places[c * width : (c + 1) * width, :], NT)
         for p in range(2):
             first, second = pack_pair(sent[:, p * LANES : (p + 1) * LANES])
-            out_ref[4 * c + 2 * p, base : base + half, :] = first
-            out_ref[4 * c + 2 * p + 1, base : base + half, :] = second
-
-
-def gather_grads(owner_count, base, got_ref, buf):
-    half = got_ref.shape[1] - base
-    own = base // 4
-    slot_count = owner_count * LANES // 2
-    for s in range(0, owner_count, 2):
-        real, imag = unpack_pair(got_ref[s, base:, :], got_ref[s + 1, base:, :])
-        lanes = pl.ds(s // 2 * LANES, LANES)
-        buf[0:half, lanes] = real
-        buf[half : 2 * half, lanes] = imag
-    total = got_ref[0, 0:base, :].astype(f32)
-    for s in range(1, owner_count):
-        total = total + got_ref[s, 0:base, :].astype(f32)
-    parts = [total[t * own : (t + 1) * own].T for t in range(4)]
-    neg = jnp.concatenate(parts, axis=0)[: 2 * half]
-    high = neg.astype(bf16)
-    buf[0 : 2 * half, slot_count : slot_count + own] = high
-    buf[0 : 2 * half, slot_count + own : slot_count + 2 * own] = (neg - high.astype(f32)).astype(bf16)
-
-
-def sum_kernel(owner_count, base, own, got_ref, asked_ref, neg_row_ref, out_ref, buf):
-    @pl.when(pl.program_id(0) == 0)
-    def _():
-        gather_grads(owner_count, base, got_ref, buf)
-
-    out_ref[...] = block_sum(own, asked_ref, neg_row_ref, buf, out_ref.shape[1])
-
-
-def block_sum(own, asked_ref, neg_row_ref, buf, rows):
-    first = pl.program_id(0) * rows
-    asked = jnp.concatenate([asked_ref[...], neg_row_ref[:, 0 : 2 * own] + 1], axis=1)
-    targets = onehot(iota((rows, asked.shape[1]), 0) + first + 1 == asked)
-    return mm(buf[...], targets, NT)
+            out_buf[4 * c + 2 * p, 0:half, :] = first
+            out_buf[4 * c + 2 * p + 1, 0:half, :] = second
+        part = pl.ds(4 * c, 4)
+        copies.append(pltpu.make_async_copy(out_buf.at[part], out_hbm.at[part], sems.at[c]))
+        copies[-1].start()
+    for copy in copies:
+        copy.wait()
+
+
+def target_kernel(mine_ref, other_ref, neg_row_ref, mine_out, other_out, neg_out):
+    for asked_ref, out in ((mine_ref, mine_out), (other_ref, other_out)):
+        slots, rows = out.shape
+        down = jnp.broadcast_to(asked_ref[...], (8, slots)).T[:, 0:1]
+        out[...] = onehot(iota((slots, rows), 1) + 1 == down)
+    count, rows = neg_out.shape
+    down = jnp.broadcast_to(neg_row_ref[...], (8, LANES)).T[:count, 0:1]
+    neg_out[...] = onehot(iota((count, rows), 1) == down)
+
+
+def sum_kernel(got_ref, targets_ref, neg_targets_ref, out_ref, buf):
+    unpack_rows(got_ref, buf)
+    neg = neg_total(got_ref, buf.shape[0])
+    rows = out_ref.shape[1]
+    width = 4 * LANES
+    for c in range(rows // width):
+        lanes = slice(c * width, (c + 1) * width)
+        out_ref[:, lanes] = mm(buf[...], targets_ref[:, lanes]) + mm(
+            neg, neg_targets_ref[:, lanes], TN
+        )
 
 
 def update_kernel(
-    owner_count, base, own,
-    got_ref, asked_ref, neg_row_ref, mine_ref, emb_ref, acc_ref, new_ref, state_ref, buf,
+    got_ref, targets_ref, neg_targets_ref, mine_ref, emb_ref, acc_ref,
+    new_hbm, state_ref, buf, new_buf, sems,
 ):
-    @pl.when(pl.program_id(0) == 0)
-    def _():
-        gather_grads(owner_count, base, got_ref, buf)
-
-    grad = mine_ref[...] + block_sum(own, asked_ref, neg_row_ref, buf, new_ref.shape[1])
-    state = acc_ref[...] + jnp.sum(grad * grad, axis=0, keepdims=True) / grad.shape[0]
-    state_ref[...] = state
-    new_ref[...] = emb_ref[...] - grad * (step_rate / jnp.sqrt(state))
-
-
-def call(kernel, outs, in_specs, scratch=(), limit=40 << 20, cost=None, **grid):
+    unpack_rows(got_ref, buf)
+    neg = neg_total(got_ref, buf.shape[0])
+    features, rows = mine_ref.shape
+    width = 4 * LANES
+    copies = []
+    for c in range(rows // width):
+        lanes = slice(c * width, (c + 1) * width)
+        other = mm(buf[...], targets_ref[:, lanes]) + mm(neg, neg_targets_ref[:, lanes], TN)
+        grad = mine_ref[:, lanes] + other
+        state = acc_ref[:, lanes] + jnp.sum(grad * grad, axis=0, keepdims=True) / features
+        state_ref[:, lanes] = state
+        new_buf[:, lanes] = emb_ref[:, lanes] - grad * (step_rate / jnp.sqrt(state))
+        part = pl.ds(c * width, width)
+        copies.append(
+            pltpu.make_async_copy(new_buf.at[:, part], new_hbm.at[:, part], sems.at[c])
+        )
+        copies[-1].start()
+    for copy in copies:
+        copy.wait()
+
+
+def call(kernel, outs, in_specs, out_specs, scratch=(), limit=20 << 20, flops=0, moved=0):
     return pl.pallas_call(
         kernel,
         out_shape=outs,
         in_specs=in_specs,
+        out_specs=out_specs,
         scratch_shapes=list(scratch),
         compiler_params=pltpu.CompilerParams(vmem_limit_bytes=limit),
-        cost_estimate=cost,
-        **grid,
-    )
-
-
-def cost(flops, moved):
-    return pl.CostEstimate(flops=flops, bytes_accessed=moved, transcendentals=0)
+        cost_estimate=pl.CostEstimate(flops=flops, bytes_accessed=moved, transcendentals=0),
+    )
 
 
 def exchange(values):
     return lax.all_to_all(values, "ent", split_axis=0, concat_axis=0, tiled=True)
+
+
+def in_hbm(values):
+    return pltpu.with_memory_space_constraint(values, pltpu.HBM)
+
+
+def swap_cores(values):
+    return lax.ppermute(values, "rep", [(0, 1), (1, 0)])
 
 
 def packed_shards(
@@ -302,11 +352,11 @@
     own = neg_ids.shape[0]
     table = embeddings.T
     shape = jax.ShapeDtypeStruct
+
     groups = LANES // own
     piece = features // groups
     pay_rows = (piece + 1 + 7) // 8 * 8
-
-    payload, place, neg_row, low_table = call(
+    requests, place, neg_row, low_table = call(
         functools.partial(request_kernel, row_count, owners, capacity, own),
         (
             shape((owners, pay_rows, LANES), bf16),
@@ -314,26 +364,31 @@
             shape((1, LANES), i32),
             shape((features, row_count), bf16),
         ),
-        [VMEM, VMEM, SMEM, VMEM, ANY],
+        [HBM] * 5,
+        (VMEM,) * 4,
         [
+            pltpu.VMEM((1, ends), i32),
+            pltpu.SMEM((own,), i32),
+            pltpu.VMEM((slot_of.shape[0] // LANES, LANES), i32),
             pltpu.VMEM((features, row_count), f32),
             pltpu.VMEM((features, LANES), f32),
-            pltpu.SemaphoreType.DMA((2,)),
+            pltpu.SemaphoreType.DMA((6,)),
         ],
-        limit=20 << 20,
     )(
-        head_ids.reshape(1, edges),
-        tail_ids.reshape(1, edges),
-        neg_ids,
-        slot_of.reshape(-1, LANES),
-        table,
-    )
-    got = exchange(payload)
+        in_hbm(head_ids.reshape(1, edges)),
+        in_hbm(tail_ids.reshape(1, edges)),
+        in_hbm(neg_ids),
+        in_hbm(slot_of.reshape(-1, LANES)),
+        in_hbm(table),
+    )
+    got = exchange(requests)
+    sems = pltpu.SemaphoreType.DMA((slots // 256,))
     answers, asked = call(
         functools.partial(answer_kernel, owners, piece),
-        (shape((owners, half, LANES), bf16), shape((1, slots), i32)),
+        (pltpu.HBM((owners, half, LANES), bf16), shape((1, slots), i32)),
         [VMEM] * 2,
-        limit=20 << 20,
+        (HBM, VMEM),
+        [pltpu.VMEM((owners, half, LANES), bf16), sems],
     )(got, low_table)
     fetched = exchange(answers)
     neg_rows = (
@@ -346,50 +401,50 @@
         relation_kernel,
         shape((features, edges), bf16),
         [VMEM] * 2,
-        limit=20 << 20,
-        cost=cost(2 * features * relations.shape[0] * edges, relations.size * 2),
+        VMEM,
+        flops=2 * features * relations.shape[0] * edges,
+        moved=relations.size * 2,
     )(rel_ids.reshape(1, edges), relations.T)
-    other_asked = lax.ppermute(asked, "rep", [(0, 1), (1, 0)])
-    base = 4 * own
+    other_asked = swap_cores(asked)
+    targets, other_targets, neg_targets = call(
+        target_kernel,
+        (
+            shape((slots, row_count), bf16),
+            shape((slots, row_count), bf16),
+            shape((2 * own, row_count), bf16),
+        ),
+        [VMEM] * 3,
+        (VMEM,) * 3,
+        flops=8 * slots * row_count,
+        moved=4 * slots * row_count,
+    )(asked, other_asked, neg_row)
+    sent_rows = half + features // LANES * own + own // 2
     outgoing = call(
-        functools.partial(edge_kernel, owners),
-        shape((owners, base + half, LANES), bf16),
-        [VMEM] * 4,
-        [pltpu.VMEM((features, slots), f32)],
-        limit=30 << 20,
-    )(fetched, rel_rows, neg_rows, place)
+        edge_kernel,
+        pltpu.HBM((owners, sent_rows, LANES), bf16),
+        [VMEM] * 5,
+        HBM,
+        [pltpu.VMEM((features, slots), bf16), pltpu.VMEM((owners, sent_rows, LANES), bf16), sems],
+    )(fetched, rel_rows, neg_rows, place, neg_targets)
     incoming = exchange(outgoing)
-    other = lax.ppermute(incoming, "rep", [(0, 1), (1, 0)])
-    block = 256
-    columns = lambda i: (0, i)
-    fixed = lambda rank: (lambda i: (0,) * rank)
-    got_specs = [
-        pl.BlockSpec((owners, base + half, LANES), fixed(3)),
-        pl.BlockSpec((1, slots), fixed(2)),
-        pl.BlockSpec((1, LANES), fixed(2)),
-    ]
-    wide = pl.BlockSpec((features, block), columns)
-    thin = pl.BlockSpec((1, block), columns)
-    buf = pltpu.VMEM((features, slots + 2 * own), bf16)
+    other = swap_cores(incoming)
+    buf = pltpu.VMEM((features, slots), bf16)
     mine = call(
-        functools.partial(sum_kernel, owners, base, own),
+        sum_kernel,
         shape((features, row_count), f32),
-        got_specs,
+        [VMEM] * 3,
+        VMEM,
         [buf],
-        limit=20 << 20,
-        cost=cost(2 * features * slots * row_count, 4 * features * row_count),
-        grid=(row_count // block,),
-        out_specs=wide,
-    )(incoming, asked, neg_row)
+        flops=2 * features * slots * row_count,
+        moved=4 * features * row_count,
+    )(incoming, targets, neg_targets)
     new_rows, new_state = call(
-        functools.partial(update_kernel, owners, base, own),
-        (shape((features, row_count), f32), shape((1, row_count), f32)),
-        got_specs + [wide, wide, thin],
-        [buf],
-        limit=20 << 20,
-        grid=(row_count // block,),
-        out_specs=(wide, thin),
-    )(other, other_asked, neg_row, mine, table, accumulator.reshape(1, row_count))
+        update_kernel,
+        (pltpu.HBM((features, row_count), f32), shape((1, row_count), f32)),
+        [VMEM] * 6,
+        (HBM, VMEM),
+        [buf, pltpu.VMEM((features, row_count), f32), pltpu.SemaphoreType.DMA((row_count // 512,))],
+    )(other, other_targets, neg_targets, mine, table, accumulator.reshape(1, row_count))
     return new_rows.T, new_state.reshape(row_count)
 
 
@@ -525,12 +580,13 @@
         4 * edges == owners * LANES // 2
         and mesh.shape["rep"] == 2
         and owners % 4 == 0
-        and LANES % negs == 0
+        and owners & (owners - 1) == 0
+        and LANES % (2 * negs) == 0
+        and negs == 16
+        and features % (LANES // negs) == 0
+        and 0 < features % LANES * 2 <= LANES
         and features % 16 == 0
-        and features <= 4 * LANES
-        and 3 * LANES < features
-        and features % (LANES // negs) == 0
-        and rows % 256 == 0
+        and rows % 512 == 0
         and rows < 256 * 255
         and entities % LANES == 0
         and entities <= 1 << 16

time: 100 us -> 91.4 us (0.914)
  waiting for transfers between devices: 16.5 us -> 10.9 us
  blocking collectives: 49.3 us -> 47.8 us
  local copies, waits for them, and re-layouts: 8.15 us -> 7.08 us
    all_to_all x1, waiting for transfers between devices: 16.5 us -> 10.6 us  [exchange(): lax.all_to_all(values, 'ent', split_axis=0, concat_axis=0, tiled=True)]
    all_to_all x2, blocking collectives: 49.3 us -> 47.8 us  [exchange(): lax.all_to_all(values, 'ent', split_axis=0, concat_axis=0, tiled=True)]
    unnamed x24 -> x20, local copies, waits for them, and re-layouts: 7.34 us -> 6.24 us
    pallas_call x5 -> x6, Pallas kernels: 17.7 us -> 17.1 us  [the longest x1 4.49 us: packed_shards(): call(update_kernel, (pltpu.HBM((features, row_count), f32), shape((1, row...]
  transfers between devices with their start and end apart: 3 -> 3, of which waited for: 1 -> 2; matrix products, arithmetic and copies ran while one was open for 1% -> 1% of each run, Pallas kernels for 6% -> 6%
where the time goes in v2:
time: 91.4 us; the launch traced here: 91 us
  blocking collectives  47.8 us (52%)
  Pallas kernels  20 us (22%)
  waiting for transfers between devices  10.9 us (12%)
  local copies, waits for them, and re-layouts  7.08 us (8%)
  starting transfers between devices  4.38 us (5%)
  between operations  0.96 us (1%)
    all_to_all x2, blocking collectives, exchange(): lax.all_to_all(values, 'ent', split_axis=0, concat_axis=0, tiled=True)  47.8 us
    all_to_all x1, waiting for transfers between devices, exchange(): lax.all_to_all(values, 'ent', split_axis=0, concat_axis=0, tiled=True)  10.6 us
    unnamed x20, local copies, waits for them, and re-layouts  6.24 us
    pallas_call x1, Pallas kernels, packed_shards(): call(update_kernel, (pltpu.HBM((features, row_count), f32), shape((1, row...  4.49 us
    pallas_call x1, Pallas kernels, packed_shards(): call(edge_kernel, pltpu.HBM((owners, sent_rows, LANES), bf16), [VMEM] * 5...  4.46 us
    all_to_all x1, starting transfers between devices, exchange(): lax.all_to_all(values, 'ent', split_axis=0, concat_axis=0, tiled=True)  4.31 us
    pallas_call x1, Pallas kernels, packed_shards(): call(functools.partial(request_kernel, row_count, owners, capacity, own),...  2.9 us
    pallas_call x1, Pallas kernels, packed_shards(): call(functools.partial(answer_kernel, owners, piece), (pltpu.HBM((owners,...  2.9 us
  transfers between devices with their start and end apart: 3, of which 2 were waited for; matrix products, arithmetic and copies ran while one was open for 1% of the time, Pallas kernels for 6%

profile of v2, /device:TPU:0, one launch (start us, length us, event | category | flops | bytes accessed | tf_op | source)
XLA Modules:
  0.0 91.0 jit_solution(7653338962150930673)
XLA Ops:
  0.6 0.0 copy-start.5
  0.6 0.0 copy-start.9
  0.7 2.9 %shard_map.95 = (bf16[16,56,128]{2,1,0:T(8,128)(2,1)S(1)}, s32[1,512]{1,0:T(1,128)S(1)}, s32[1,128]{1,0:T(1,128)S(1)}, bf16[400,2048]{1,0:T(8,128)(2,1)S(1)}) custom-call(s32[1,256]{1,0:T(1,128)} %bitcast.23, s32[1,256]{1,0:T(1,128)} %bitcast.24, s32[16]{0:T(128)} %neg_hbm.1, s32[256,128]{1,0:T(8,128)} %bitcast.22, f32[400,2048]{1,0:T(8,128)} %bitcast.15), custom_call_target="tpu_custom_call" | custom-call | tf_op jit(solution)/shard_map/pallas_call | solution.py:359
  3.6 17.4 %all_to_all.15.got_ref = bf16[16,56,128]{2,1,0:T(8,128)(2,1)S(1)} all-to-all(bf16[16,56,128]{2,1,0:T(8,128)(2,1)S(1)} %get-tuple-element.13), channel_id=1, replica_groups=mesh['ent'=16,'rep'=2] {'ent'}, dimensions={0} | all-to-all | bytes 458752 | tf_op jit(solution)/shard_map/all_to_all | solution.py:331
  21.0 2.9 %shard_map.96 = (bf16[16,200,128]{2,1,0:T(8,128)(2,1)}, s32[1,1024]{1,0:T(1,128)S(1)}) custom-call(bf16[16,56,128]{2,1,0:T(8,128)(2,1)S(1)} %all_to_all.15.got_ref, bf16[400,2048]{1,0:T(8,128)(2,1)S(1)} %get-tuple-element.14.table_ref), custom_call_target="tpu_custom_call" | custom-call | tf_op jit(solution)/shard_map/pallas_call | solution.py:386
  23.9 4.3 %all-to-all-start.1 = ((bf16[16,200,128]{2,1,0:T(8,128)(2,1)}), bf16[16,200,128]{2,1,0:T(8,128)(2,1)}, u32[]{:S(2)}, u32[]{:S(2)}) async-start(bf16[16,200,128]{2,1,0:T(8,128)(2,1)} %get-tuple-element.15), calls=%async_computation.1 | async-start | bytes 1638400 | tf_op jit(solution)/shard_map/all_to_all | solution.py:331
  28.2 0.1 collective-permute-start
  28.3 0.0 copy-done.5
  28.3 0.0 copy-done.9
  28.3 1.0 %shard_map.97.rel_ref = bf16[400,256]{1,0:T(8,128)(2,1)S(1)} custom-call(s32[1,256]{1,0:T(1,128)S(1)} %bitcast.20, bf16[400,4096]{1,0:T(8,128)(2,1)S(1)} %bitcast.17), custom_call_target="tpu_custom_call" | custom-call | flops 838860800 | bytes 3276800 | tf_op jit(solution)/shard_map/pallas_call | solution.py:400
  29.3 0.0 copy-start.6
  29.3 0.7 copy-done.6
  30.0 0.3 copy.11
  30.3 0.1 copy.12
  30.5 0.4 reshape.33.neg_ref
  30.8 0.0 collective-permute-done.other_ref
  30.8 1.8 %shard_map.98 = (bf16[1024,2048]{1,0:T(8,128)(2,1)S(1)}, bf16[1024,2048]{1,0:T(8,128)(2,1)S(1)}, bf16[32,2048]{1,0:T(8,128)(2,1)S(1)}) custom-call(s32[1,1024]{1,0:T(1,128)S(1)} %get-tuple-element.17.mine_ref, s32[1,1024]{1,0:T(1,128)S(1)} %collective-permute-done.other_ref, s32[1,128]{1,0:T(1,128)S(1)} %get-tuple-element.18.neg_row_ref), custom_call_target="tpu_custom_call" | custom-call | flops 16777216 | bytes 8388608 | tf_op jit(solution)/shard_map/pallas_call | solution.py:409
  32.7 0.0 copy-start.1
  32.7 2.0 %copy-done.1 = bf16[1024,2048]{1,0:T(8,128)(2,1)} copy-done((bf16[1024,2048]{1,0:T(8,128)(2,1)}, bf16[1024,2048]{1,0:T(8,128)(2,1)S(1)}, u32[]{:S(2)}) %copy-start.1) | copy-done | bytes 4194328
  34.6 0.0 copy-start.3
  34.6 2.0 %copy-done.3 = bf16[1024,2048]{1,0:T(8,128)(2,1)} copy-done((bf16[1024,2048]{1,0:T(8,128)(2,1)}, bf16[1024,2048]{1,0:T(8,128)(2,1)S(1)}, u32[]{:S(2)}) %copy-start.3) | copy-done | bytes 4194328
  36.6 10.6 %all-to-all-done.1.got_ref = bf16[16,200,128]{2,1,0:T(8,128)(2,1)} async-done(((bf16[16,200,128]{2,1,0:T(8,128)(2,1)}), bf16[16,200,128]{2,1,0:T(8,128)(2,1)}, u32[]{:S(2)}, u32[]{:S(2)}) %all-to-all-start.1) | async-done | bytes 819232 | tf_op jit(solution)/shard_map/all_to_all | solution.py:331
  47.2 0.0 copy-start.4
  47.2 0.0 copy-start.7
  47.2 1.1 %copy-done.7 = bf16[400,256]{1,0:T(8,128)(2,1)S(1)} copy-done((bf16[400,256]{1,0:T(8,128)(2,1)S(1)}, bf16[400,256]{1,0:T(8,128)(2,1)}, u32[]{:S(2)}) %copy-start.7) | copy-done | bytes 204824
  48.3 4.5 %shard_map.99 = bf16[16,256,128]{2,1,0:T(8,128)(2,1)} custom-call(bf16[16,200,128]{2,1,0:T(8,128)(2,1)} %all-to-all-done.1.got_ref, bf16[400,256]{1,0:T(8,128)(2,1)S(1)} %copy-done.7, bf16[256,400]{1,0:T(8,128)(2,1)S(1)} %reshape.33.neg_ref, s32[1,512]{1,0:T(1,128)S(1)} %get-tuple-element.16.place_ref, bf16[32,2048]{1,0:T(8,128)(2,1)S(1)} %get-tuple-element.19._.neg_targets_ref), custom_call_target="tpu_custom_call" | custom-call | tf_op jit(solution)/shard_map/pallas_call | solution.py:422
  52.8 30.4 %all_to_all.16.got_ref = bf16[16,256,128]{2,1,0:T(8,128)(2,1)S(1)} all-to-all(bf16[16,256,128]{2,1,0:T(8,128)(2,1)} %shard_map.99), channel_id=1, replica_groups=mesh['ent'=16,'rep'=2] {'ent'}, dimensions={0} | all-to-all | bytes 2097152 | tf_op jit(solution)/shard_map/all_to_all | solution.py:331
  83.2 0.0 collective-permute-start.1
  83.2 0.0 copy-done.4
  83.2 0.0 copy-start
  83.2 0.0 copy-start.2
  83.2 0.0 copy-start.8
  83.2 2.4 %shard_map.100.mine_ref = f32[400,2048]{1,0:T(8,128)S(1)} custom-call(bf16[16,256,128]{2,1,0:T(8,128)(2,1)S(1)} %all_to_all.16.got_ref, bf16[1024,2048]{1,0:T(8,128)(2,1)S(1)} %copy-done.4, bf16[32,2048]{1,0:T(8,128)(2,1)S(1)} %get-tuple-element.19._.neg_targets_ref), custom_call_target="tpu_custom_call" | custom-call | flops 1677721600 | bytes 3276800 | tf_op jit(solution)/shard_map/pallas_call | solution.py:432
  85.6 0.2 collective-permute-done.1.got_ref
  85.9 0.0 copy-done
  85.9 0.5 copy-done.2
  86.4 0.0 copy-done.8
  86.4 4.5 %shard_map.101 = (f32[400,2048]{1,0:T(8,128)}, f32[1,2048]{1,0:T(1,128)}) custom-call(bf16[16,256,128]{2,1,0:T(8,128)(2,1)S(1)} %collective-permute-done.1.got_ref, bf16[1024,2048]{1,0:T(8,128)(2,1)S(1)} %copy-done.2, bf16[32,2048]{1,0:T(8,128)(2,1)S(1)} %get-tuple-element.19._.neg_targets_ref, f32[400,2048]{1,0:T(8,128)S(1)} %shard_map.100.mine_ref, ...), custom_call_target="tpu_custom_call" | custom-call | tf_op jit(solution)/shard_map/pallas_call | solution.py:441
Async XLA Ops:
  0.6 27.6 %copy-start.5 = (bf16[4096,400]{0,1:T(8,128)(2,1)S(1)}, bf16[4096,400]{0,1:T(8,128)(2,1)}, u32[]{:S(2)}) copy-start(bf16[4096,400]{0,1:T(8,128)(2,1)} %param.13) | copy-start | bytes 9830404
  0.6 27.6 %copy-start.9 = (s32[256]{0:T(256)S(1)}, s32[256]{0:T(256)}, u32[]{:S(2)}) copy-start(s32[256]{0:T(256)} %param.9) | copy-start | bytes 3076
  23.9 23.4 %all-to-all-start.1 = ((bf16[16,200,128]{2,1,0:T(8,128)(2,1)}), bf16[16,200,128]{2,1,0:T(8,128)(2,1)}, u32[]{:S(2)}, u32[]{:S(2)}) async-start(bf16[16,200,128]{2,1,0:T(8,128)(2,1)} %get-tuple-element.15), calls=%async_computation.1 | async-start | bytes 1638400 | tf_op jit(solution)/shard_map/all_to_all | solution.py:331
  28.2 2.7 %collective-permute-start = (s32[1,1024]{1,0:T(1,128)S(1)}, s32[1,1024]{1,0:T(1,128)S(1)}, u32[]{:S(2)}, u32[]{:S(2)}) collective-permute-start(s32[1,1024]{1,0:T(1,128)S(1)} %get-tuple-element.17.mine_ref), channel_id=1, source_target_pairs={{0,1},{1,0},{2,3},{3,2},{4,5},{5,4},{6,7},{7,6},{8,9},{9,8},{10,11... | collective-permute-start | bytes 12296 | tf_op jit(solution)/shard_map/ppermute | solution.py:339
  29.3 0.7 copy-start.6
  32.7 2.0 %copy-start.1 = (bf16[1024,2048]{1,0:T(8,128)(2,1)}, bf16[1024,2048]{1,0:T(8,128)(2,1)S(1)}, u32[]{:S(2)}) copy-start(bf16[1024,2048]{1,0:T(8,128)(2,1)S(1)} %get-tuple-element.20.targets_ref) | copy-start | bytes 12582916
  34.6 2.0 %copy-start.3 = (bf16[1024,2048]{1,0:T(8,128)(2,1)}, bf16[1024,2048]{1,0:T(8,128)(2,1)S(1)}, u32[]{:S(2)}) copy-start(bf16[1024,2048]{1,0:T(8,128)(2,1)S(1)} %get-tuple-element.21.targets_ref) | copy-start | bytes 12582916
  47.2 36.0 %copy-start.4 = (bf16[1024,2048]{1,0:T(8,128)(2,1)S(1)}, bf16[1024,2048]{1,0:T(8,128)(2,1)}, u32[]{:S(2)}) copy-start(bf16[1024,2048]{1,0:T(8,128)(2,1)} %copy-done.3) | copy-start | bytes 12582916
  47.2 1.1 %copy-start.7 = (bf16[400,256]{1,0:T(8,128)(2,1)S(1)}, bf16[400,256]{1,0:T(8,128)(2,1)}, u32[]{:S(2)}) copy-start(bf16[400,256]{1,0:T(8,128)(2,1)} %copy-done.6) | copy-start | bytes 614404
  83.2 2.7 %collective-permute-start.1 = (bf16[16,256,128]{2,1,0:T(8,128)(2,1)S(1)}, bf16[16,256,128]{2,1,0:T(8,128)(2,1)S(1)}, u32[]{:S(2)}, u32[]{:S(2)}) collective-permute-start(bf16[16,256,128]{2,1,0:T(8,128)(2,1)S(1)} %all_to_all.16.got_ref), channel_id=1, source_target_pairs={{0,1},{1,0},{2,3},{3,2},{4,5},{5,4},{6,7},{7,6},{8,9},{9,8},{10,11... | collective-permute-start | bytes 3145736 | tf_op jit(solution)/shard_map/ppermute | solution.py:339
  83.2 2.7 %copy-start = (f32[2048,400]{0,1:T(8,128)S(1)}, f32[2048,400]{0,1:T(8,128)}, u32[]{:S(2)}) copy-start(f32[2048,400]{0,1:T(8,128)} %param.14) | copy-start | bytes 9830404
  83.2 3.2 %copy-start.2 = (bf16[1024,2048]{1,0:T(8,128)(2,1)S(1)}, bf16[1024,2048]{1,0:T(8,128)(2,1)}, u32[]{:S(2)}) copy-start(bf16[1024,2048]{1,0:T(8,128)(2,1)} %copy-done.1) | copy-start | bytes 12582916
  83.2 3.2 %copy-start.8 = (f32[2048]{0:T(1024)S(1)}, f32[2048]{0:T(1024)}, u32[]{:S(2)}) copy-start(f32[2048]{0:T(1024)} %param.15) | copy-start | bytes 24580
